TPU v7x, 32 devices: a whole 2x2x4 slice. The times are simulated.
32 devices in a mesh: groups: 1, samp: 4 (over x, core), var: 8 (over z, y).
Axes of the slice: x: 2, y: 2, z: 4, core: 2. Of those that a mesh axis runs over, the one named last changes fastest.
Arguments:
- expression: bfloat16 [4096, 5120], P(('groups', 'samp'), 'var'), may hold values from -6 to 6
- genotypes: bfloat16 [4096, 1536], P(('groups', 'samp'), 'var'), may hold values from 0 to 2
- covariates: bfloat16 [4096, 64], P(('groups', 'samp')), may hold values from -6 to 6
- distance_bins: int32 [24, 5120], P('groups', ('var', 'samp')), may hold values from 0 to 15
- gene_folds: int32 [5120], P(('groups', 'var', 'samp')), may hold values from 0 to 4
- fold_weights: float32 [5, 16], replicated, may hold values from 0.25 to 4
Outputs:
- weighted_stats: float32 [5120, 1536], P(('groups', 'var', 'samp'))
Inputs may be any that keep to these rules, and one draw needn't show every extreme that they name: `distance_bins`: bins index rows of fold_weights' second dimension. `gene_folds`: folds index rows of fold_weights.
All inputs are finite; a program needn't handle non-finite values.
Results may differ from a plain program's by a relative error of at most 0.0047.
Values may be sent and summed in bfloat16 or wider, within the bound.
A program may use at most 64 MiB of HBM per device.

v0:
```python
import jax
import jax.numpy as jnp
from jax import lax
from jax.sharding import PartitionSpec as P

COVS = 64
VARS = 1536
VTILE = 64
NBINS = 16
FOLDS = 5
VTILES = 24


def solve_fit(data, design, factor, cross):
    beta = jax.scipy.linalg.cho_solve((factor, True), cross)
    fitted = jnp.dot(design.astype(jnp.float32), beta, precision=lax.Precision.HIGHEST)
    return (beta, data.astype(jnp.float32) - fitted)


def shards(expression, genotypes, covariates, distance_bins, gene_folds, fold_weights):
    sample_rows = expression.shape[0]
    samples = sample_rows * lax.axis_size("samp")
    design = jnp.concatenate([jnp.ones((sample_rows, 1), jnp.bfloat16), covariates], axis=1)
    source = lax.all_gather(genotypes, "var", axis=1, tiled=True)
    gram = jnp.dot(design.T, design, preferred_element_type=jnp.float32)
    expr_cross = jnp.dot(design.T, expression, preferred_element_type=jnp.float32)
    geno_cross = jnp.dot(design.T, source, preferred_element_type=jnp.float32)
    partial_sums = (gram, expr_cross, geno_cross)
    summed = lax.psum((partial_sums[0], partial_sums[1], partial_sums[2]), "samp")
    gram, expr_cross, geno_cross = (summed[0], summed[1], summed[2])
    factor = jnp.linalg.cholesky(gram)
    expr_beta, expr_resid = solve_fit(expression, design, factor, expr_cross)
    geno_beta, geno_resid = solve_fit(source, design, factor, geno_cross)
    expr_norm, geno_norm = lax.psum(
        (jnp.sum(expr_resid * expr_resid, axis=0), jnp.sum(geno_resid * geno_resid, axis=0)), "samp"
    )
    expr_unit = (expr_resid * lax.rsqrt(expr_norm + 1e-06)).astype(jnp.bfloat16)
    geno_unit = (geno_resid * lax.rsqrt(geno_norm + 1e-06)).astype(jnp.bfloat16)
    terms = lax.dot_general(
        expr_unit, geno_unit, (((0,), (0,)), ((), ())), preferred_element_type=jnp.float32
    )
    corr = lax.psum_scatter(terms, "samp", scatter_dimension=0, tiled=True)
    local_genes = corr.shape[0]
    fold_onehot = (gene_folds[:, None] == jnp.arange(FOLDS)[None, :]).astype(jnp.float32)
    row_weights = jnp.dot(fold_onehot, fold_weights, precision=lax.Precision.HIGHEST)
    bin_match = distance_bins.T[:, :, None] == jnp.arange(NBINS)[None, None, :]
    tile_weight = jnp.sum(jnp.where(bin_match, row_weights[:, None, :], 0.0), axis=2)
    dof = jnp.float32(samples - COVS - 2)
    stats = dof * corr * corr
    weighted = stats.reshape(local_genes, VTILES, VTILE) * tile_weight[:, :, None]
    return weighted.reshape(local_genes, VARS)


def solution(mesh):
    return jax.shard_map(
        shards,
        mesh=mesh,
        in_specs=(
            P(("groups", "samp"), "var"),
            P(("groups", "samp"), "var"),
            P(("groups", "samp"), None),
            P("groups", ("var", "samp")),
            P(("groups", "var", "samp")),
            P(),
        ),
        out_specs=P(("groups", "var", "samp"), None),
        check_vma=False,
    )
```

profile of v0, /device:TPU:13, one launch (start us, length us, event | category | flops | bytes accessed | tf_op | source)
XLA Modules:
  0.0 190.1 jit_solution(71797673533566679)
XLA Ops:
  6.5 0.7 all-gather.2.cloned.1.call-update
  7.3 0.0 all-reduce.5.cloned.1.call-start
  7.3 1.2 fusion.11
  8.5 10.7 %psum.35 = f32[65,65]{0,1:T(8,128)S(1)} all-reduce(f32[65,65]{0,1:T(8,128)S(1)} %fusion.11), channel_id=1, replica_groups=mesh['groups'=1,'samp'=4,'var'=8] {'samp'}, use_global_device_ids=true, to_apply=%region_0.0 | all-reduce | flops 4225 | bytes 33800 | tf_op jit(solution)/shard_map/psum | solution.py:29
  19.2 0.1 copy.23
  19.3 5.9 %cholesky.16 = f32[65,65]{1,0:T(8,128)S(1)} custom-call(f32[65,65]{1,0:T(8,128)S(1)} %fusion.24), custom_call_target="Cholesky" | custom-call | tf_op jit(solution)/shard_map/jit(cholesky)/cholesky | solution.py:31
  25.3 2.4 %fusion.9 = f32[65,640]{1,0:T(8,128)} fusion(bf16[1024,640]{1,0:T(8,128)(2,1)} %param.6, bf16[1024,64]{0,1:T(8,128)(2,1)} %param.8), kind=kOutput, calls=%fused_computation.18 | convolution fusion | flops 85196800 | bytes 1608192 | tf_op jit(solution)/shard_map/dot_general | solution.py:26
  27.7 40.7 %all-gather.2.cloned.1.call-done = bf16[1024,1536]{0,1:T(8,128)(2,1)} async-done(((bf16[1024,192]{0,1:T(8,128)(2,1)}), bf16[1024,1536]{0,1:T(8,128)(2,1)}) %all-gather.2.cloned.1.call-update) | async-done | bytes 3145744 | tf_op jit(solution)/shard_map/all_gather | solution.py:24
  68.4 4.0 %fusion.5 = f32[65,1536]{1,0:T(8,128)} fusion(bf16[1024,1536]{0,1:T(8,128)(2,1)} %all-gather.2.cloned.1.call-done, bf16[1024,64]{0,1:T(8,128)(2,1)} %param.8), kind=kOutput, calls=%fused_computation.14 | convolution fusion | flops 204472320 | bytes 3676160 | tf_op jit(solution)/shard_map/dot_general | solution.py:27
  72.3 0.0 reduce-scatter.2.cloned.1.call-start
  72.4 0.7 compare_reduce_fusion
  73.1 0.6 fusion.15
  73.7 5.0 %custom-call.16 = f32[1,65,65]{1,2,0:T(8,128)S(1)} custom-call(f32[1,65,65]{2,1,0:T(8,128)S(1)} %fusion.15), custom_call_target="InvertDiagBlocksLowerTriangular" | custom-call | tf_op jit(solution)/shard_map/jit(_cho_solve)/triangular_solve | solution.py:15
  78.7 3.0 %copy.24 = bf16[1024,1536]{1,0:T(8,128)(2,1)} copy(bf16[1024,1536]{0,1:T(8,128)(2,1)S(1)} %copy-done.1) | data formatting | bytes 6291456 | tf_op jit(solution)/shard_map/all_gather | solution.py:24
  81.7 25.1 %all-reduce.5.cloned.1.call-done = (f32[65,1536]{1,0:T(8,128)}, f32[65,640]{1,0:T(8,128)}) async-done(((f32[65,1536]{1,0:T(8,128)}, f32[65,640]{1,0:T(8,128)}), (f32[65,1536]{1,0:T(8,128)}, f32[65,640]{1,0:T(8,128)})) %all-reduce.5.cloned.1.call-update) | async-done | bytes 565776 | tf_op jit(solution)/shard_map/psum | solution.py:29
  106.8 1.6 fusion.18
  108.3 0.5 fusion.16
  108.9 1.4 fusion.22
  110.3 0.3 fusion.20
  110.7 3.0 %multiply_reduce_fusion.1 = (f32[640]{0:T(1024)S(1)}, f32[1024,640]{1,0:T(8,128)}) fusion(bf16[1024,640]{1,0:T(8,128)(2,1)S(1)} %copy-done.3, f32[65,640]{1,0:T(8,128)S(1)} %fusion.20, bf16[1024,64]{0,1:T(8,128)(2,1)S(1)} %copy-done.4), kind=kOutput, calls=%fused_computation.6 | convolution fusion | flops 513801600 | bytes 4232192 | tf_op jit(solution)/shard_map/dot_general | solution.py:16
  113.6 5.1 %multiply_reduce_fusion = (f32[1536]{0:T(1024)S(1)}, f32[1024,1536]{1,0:T(8,128)}) fusion(f32[65,1536]{1,0:T(8,128)S(1)} %fusion.16, bf16[1024,64]{0,1:T(8,128)(2,1)S(1)} %copy-done.4, bf16[1024,1536]{1,0:T(8,128)(2,1)S(1)} %copy-done.2), kind=kOutput, calls=%fused_computation.1 | convolution fusion | flops 1233123840 | bytes 9973760 | tf_op jit(solution)/shard_map/dot_general | solution.py:16
  118.7 10.2 %all-reduce.1 = (f32[1536]{0:T(1024)S(1)}, f32[640]{0:T(1024)S(1)}) all-reduce(f32[1536]{0:T(1024)S(1)} %get-tuple-element.9, f32[640]{0:T(1024)S(1)} %get-tuple-element.11), channel_id=1, replica_groups=mesh['groups'=1,'samp'=4,'var'=8] {'samp'}, use_global_device_ids=true, to_apply=%region_8.9 | all-reduce | flops 2176 | bytes 17408 | tf_op jit(solution)/shard_map/psum | solution.py:34
  129.0 7.9 %fusion = f32[640,1536]{1,0:T(8,128)} fusion(f32[1024,1536]{1,0:T(8,128)} %get-tuple-element.10, f32[1536]{0:T(1024)S(1)} %add_rsqrt_fusion, f32[1024,640]{1,0:T(8,128)} %get-tuple-element.12, bf16[1024,640]{1,0:T(8,128)(2,1)S(1)} %copy-done.3, f32[640]{0:T(1024)S(1)} %add_rsqrt_fusion.1), kind=kOutput, calls=%fused_computation.3 | convolution fusion | flops 2019033088 | bytes 14164480 | tf_op jit(solution)/shard_map/dot_general | solution.py:39
  136.9 0.6 copy-done.6
  137.5 0.2 fusion.13
  137.7 0.0 copy-done.5
  137.7 0.1 select_reduce_fusion
  137.9 0.1 copy.25
  138.0 0.6 mul.51
  138.5 0.5 mul.52
  139.0 42.2 %reduce-scatter.2.cloned.1.call-done = f32[160,1536]{1,0:T(8,128)} async-done(((f32[640,1536]{1,0:T(8,128)}), f32[160,1536]{1,0:T(8,128)}) %reduce-scatter.2.cloned.1.call-update) | async-done | bytes 983056 | tf_op jit(solution)/shard_map/reduce_scatter | solution.py:42
  181.2 2.3 %fusion.3 = f32[160,1536]{1,0:T(8,128)} fusion(f32[160,1536]{1,0:T(8,128)S(1)} %mul.52, f32[160,1536]{1,0:T(8,128)} %reduce-scatter.2.cloned.1.call-done), kind=kLoop, calls=%fused_computation.10 | loop fusion | flops 737280 | bytes 2949120 | tf_op jit(solution)/shard_map/mul | solution.py:50
  (19 shorter events, 0.1 us)
Async XLA Ops:
  6.5 130.3 %copy-start = (f32[5,16]{1,0:T(8,128)S(1)}, f32[5,16]{1,0:T(8,128)}, u32[]{:S(2)}) copy-start(f32[5,16]{1,0:T(8,128)} %param.11) | copy-start | bytes 964
  6.5 61.8 %all-gather.2.cloned.1.call-start = ((), (), s32[]{:S(2)}) async-start(), calls=%async_computation.1 | async-start | bytes 3538944 | tf_op jit(solution)/shard_map/all_gather | solution.py:24
  7.3 99.5 %all-reduce.5.cloned.1.call-start = ((), (), s32[]{:S(2)}) async-start(), calls=%async_computation.3 | async-start | bytes 1253376 | tf_op jit(solution)/shard_map/psum | solution.py:29
  68.4 10.3 %copy-start.1 = (bf16[1024,1536]{0,1:T(8,128)(2,1)S(1)}, bf16[1024,1536]{0,1:T(8,128)(2,1)}, u32[]{:S(2)}) copy-start(bf16[1024,1536]{0,1:T(8,128)(2,1)} %all-gather.2.cloned.1.call-done) | copy-start | bytes 9437188
  72.3 108.9 %reduce-scatter.2.cloned.1.call-start = ((), (), s32[]{:S(2)}) async-start(), calls=%async_computation.2 | async-start | bytes 4915200 | tf_op jit(solution)/shard_map/reduce_scatter | solution.py:42
  81.7 29.0 %copy-start.3 = (bf16[1024,640]{1,0:T(8,128)(2,1)S(1)}, bf16[1024,640]{1,0:T(8,128)(2,1)}, u32[]{:S(2)}) copy-start(bf16[1024,640]{1,0:T(8,128)(2,1)} %param.6) | copy-start | bytes 3932164
  81.7 29.0 %copy-start.4 = (bf16[1024,64]{0,1:T(8,128)(2,1)S(1)}, bf16[1024,64]{0,1:T(8,128)(2,1)}, u32[]{:S(2)}) copy-start(bf16[1024,64]{0,1:T(8,128)(2,1)} %param.8) | copy-start | bytes 393220
  108.8 4.8 %copy-start.2 = (bf16[1024,1536]{1,0:T(8,128)(2,1)S(1)}, bf16[1024,1536]{1,0:T(8,128)(2,1)}, u32[]{:S(2)}) copy-start(bf16[1024,1536]{1,0:T(8,128)(2,1)} %copy.24) | copy-start | bytes 9437188
  136.8 0.7 copy-start.6
  136.8 0.9 copy-start.5
Sparse Core Ops, SparseCore 0:
  9.5 58.8 all-gather.1
  72.5 34.2 all-reduce.4
  137.0 44.2 reduce-scatter.1
where the time goes:
time: 192 us; the launch traced here: 190 us
  waiting for transfers between devices  109 us (57%)
  matrix products  27.5 us (14%)
  blocking collectives  20.9 us (11%)
  other arithmetic  14.7 us (8%)
  between operations  13.2 us (7%)
  local copies, waits for them, and re-layouts  4.89 us (3%)
    reduce_scatter x1, waiting for transfers between devices, shards(): corr = lax.psum_scatter(terms, 'samp', scatter_dimension=0, tiled=True)  42.2 us
    all_gather x1, waiting for transfers between devices, shards(): source = lax.all_gather(genotypes, 'var', axis=1, tiled=True)  40.7 us
    psum x1, waiting for transfers between devices, shards(): lax.psum((partial_sums[0], partial_sums[1], partial_sums[2]), 'samp')  25.1 us
    psum x1, blocking collectives, shards(): lax.psum((partial_sums[0], partial_sums[1], partial_sums[2]), 'samp')  10.7 us
    psum x1, blocking collectives, shards(): lax.psum((jnp.sum(expr_resid * expr_resid, axis=0), jnp.sum(geno_resid *...  10.2 us
    dot_general x2, matrix products, solve_fit(): jnp.dot(design.astype(jnp.float32), beta, precision=lax.Precision.HIGHEST)  8.07 us
    dot_general x1, matrix products, shards(): lax.dot_general(expr_unit, geno_unit, (((0,), (0,)), ((), ())), preferred...  7.85 us
    another operation x3, other arithmetic, shards(): factor = jnp.linalg.cholesky(gram)  6.64 us
  transfers between devices with their start and end apart: 3, of which 3 were waited for; matrix products, arithmetic and copies ran while one was open for 11% of the time, Pallas kernels for 0%

commit v1 on v0

v1 whole, which is shorter than its diff:
```python
import functools
import math
import jax
import jax.numpy as jnp
from jax import lax
from jax.experimental import pallas as pl
from jax.experimental.pallas import tpu as pltpu
from jax.sharding import PartitionSpec as P

COVS = 64
VARS = 1536
VTILE = 64
NBINS = 16
FOLDS = 5
VTILES = 24
LANES = 128
MESH = pl.DeviceIdType.MESH
NT = (((1,), (1,)), ((), ()))
NN = (((1,), (0,)), ((), ()))


def round_up(size, step):
    return -(-size // step) * step


DESIGN = COVS + 1
DROWS = round_up(DESIGN, 8)


def remote(src, dst, send, recv, axis, peer):
    return pltpu.make_async_remote_copy(
        src_ref=src, dst_ref=dst, send_sem=send, recv_sem=recv,
        device_id={axis: peer}, device_id_type=MESH,
    )


def invert(gram):
    rows = lax.broadcasted_iota(jnp.int32, gram.shape, 0)
    cols = lax.broadcasted_iota(jnp.int32, gram.shape, 1)
    valid = (rows < DESIGN) & (cols < DESIGN)
    start = jnp.where(valid, gram, 0.0)

    def sweep(k, a):
        row = jnp.sum(jnp.where(rows == k, a, 0.0), axis=0, keepdims=True)
        col = jnp.sum(jnp.where(cols == k, a, 0.0), axis=1, keepdims=True)
        pivot = jnp.sum(jnp.where(cols[:1] == k, row, 0.0), axis=1, keepdims=True)
        inv = 1.0 / pivot
        scaled = row * inv
        a = jnp.where(cols == k, 0.0, a) - col * jnp.where(cols[:1] == k, inv, scaled)
        return jnp.where(rows == k, jnp.where(cols[:1] == k, inv, scaled), a)

    swept = lax.fori_loop(0, DESIGN, sweep, start)
    return jnp.where(valid, swept, 0.0)


def kernel(S, V, xe_ref, xg_ref, gt_ref, d_ref, out_ref,
           gbuf, bbuf, btile, bsend, gram_own, gram_in, cross_own, cross_in,
           resid, norm_own, norm_in, norm_cols, unit, source, terms, terms_in,
           gs, gr, bs, br, ms, mr, cs, cr, ns, nr, ts, tr):
    me = lax.axis_index("var")
    mine = lax.axis_index("samp")
    genes, samples = xe_ref.shape
    vb = gt_ref.shape[0]
    etiles = genes // LANES
    gtiles = xg_ref.shape[0] // LANES
    tiles = etiles + gtiles
    groups, group = terms.shape[0], terms.shape[2] // vb
    chunk = genes // S

    def var_peer(k):
        return lax.rem(me + k, V)

    def samp_peer(k):
        return lax.rem(mine + k, S)

    barrier = pltpu.get_barrier_semaphore()
    for k in range(1, V):
        pl.semaphore_signal(barrier, inc=1, device_id={"var": var_peer(k)}, device_id_type=MESH)
    for k in range(1, S):
        pl.semaphore_signal(barrier, inc=1, device_id={"samp": samp_peer(k)}, device_id_type=MESH)
    gram = lax.dot_general(d_ref[...], d_ref[...], NT, preferred_element_type=jnp.float32)
    gram_own[...] = gram[:DROWS]
    norm_own[...] = jnp.zeros_like(norm_own)
    pl.semaphore_wait(barrier, V + S - 2)

    def block_copy(k):
        return remote(gt_ref, gbuf.at[me], gs.at[k], gr.at[me], "var", var_peer(k))

    def gram_copy(k):
        return remote(gram_own, gram_in.at[mine], ms.at[k], mr.at[mine], "samp", samp_peer(k))

    def cross_copy(k):
        return remote(cross_own, cross_in.at[mine], cs.at[k], cr.at[mine], "samp", samp_peer(k))

    def norm_copy(k):
        return remote(norm_own, norm_in.at[mine], ns.at[k], nr.at[mine], "samp", samp_peer(k))

    def beta_copy(k):
        return remote(bsend, bbuf.at[me], bs.at[k], br.at[me], "var", var_peer(k))

    for k in range(1, S):
        gram_copy(k).start()
    for k in range(1, V):
        block_copy(k).start()

    def x_tile(t, use):
        @pl.when(t < etiles)
        def _():
            use(xe_ref[pl.ds(pl.multiple_of(t * LANES, LANES), LANES), :])

        @pl.when(t >= etiles)
        def _():
            use(xg_ref[pl.ds(pl.multiple_of((t - etiles) * LANES, LANES), LANES), :])

    @pl.loop(0, tiles)
    def _(t):
        def use(x):
            full = lax.dot_general(d_ref[...], x, NT, preferred_element_type=jnp.float32)
            cross_own[t] = full[:DROWS]
        x_tile(t, use)

    for k in range(1, S):
        cross_copy(k).start()
    gbuf[me] = gt_ref[...]

    gram_sum = gram_own[...]
    for k in range(1, S):
        p = samp_peer(k)
        remote(gram_own, gram_in.at[p], ms.at[k], mr.at[p], "samp", p).wait_recv()
        gram_sum = gram_sum + gram_in[p]
    inverse = invert(gram_sum)
    inverse = jnp.concatenate([inverse, jnp.zeros((LANES - DROWS, LANES), jnp.float32)], axis=0)

    for k in range(1, S):
        p = samp_peer(k)
        remote(cross_own, cross_in.at[p], cs.at[k], cr.at[p], "samp", p).wait_recv()

    @pl.loop(0, tiles)
    def _(t):
        total = cross_own[t]
        for k in range(1, S):
            total = total + cross_in[samp_peer(k), t]
        padded = jnp.concatenate([total, jnp.zeros((LANES - DROWS, LANES), jnp.float32)], axis=0)
        beta = lax.dot_general(padded.T, inverse, NN, precision=lax.Precision.HIGHEST,
                               preferred_element_type=jnp.float32)
        hi = beta.astype(jnp.bfloat16)
        lo = (beta - hi.astype(jnp.float32)).astype(jnp.bfloat16)
        fitted = lax.dot_general(hi, d_ref[...], NN, preferred_element_type=jnp.float32)
        fitted = fitted + lax.dot_general(lo, d_ref[...], NN, preferred_element_type=jnp.float32)

        def use(x):
            left = x.astype(jnp.float32) - fitted
            resid[t] = left
            square = left * left
            part = square[:, :LANES]
            for c in range(1, samples // LANES):
                part = part + square[:, c * LANES:(c + 1) * LANES]
            norm_own[pl.ds(t, 1), :] = jnp.sum(part.T, axis=0, keepdims=True)
        x_tile(t, use)

        @pl.when(t >= etiles)
        def _():
            btile[t - etiles] = hi

    for k in range(1, S):
        norm_copy(k).start()
    norm = norm_own[...]
    for k in range(1, S):
        p = samp_peer(k)
        remote(norm_own, norm_in.at[p], ns.at[k], nr.at[p], "samp", p).wait_recv()
        norm = norm + norm_in[p]
    norm_cols[...] = lax.rsqrt(norm + 1e-06)

    def column(t):
        row = norm_cols[pl.ds(t, 1), :]
        return jnp.broadcast_to(row, (LANES, LANES)).T

    lanes = lax.broadcasted_iota(jnp.int32, (LANES, LANES), 1)
    for g in range(gtiles):
        col = column(etiles + g)
        hi = col.astype(jnp.bfloat16).astype(jnp.float32)
        lo = col - hi
        message = btile[g].astype(jnp.float32)
        message = jnp.where(lanes == DESIGN, hi, jnp.where(lanes == DESIGN + 1, lo, message))
        rows = min(LANES, vb - g * LANES)
        bsend[pl.ds(g * LANES, rows), :] = message[:rows].astype(jnp.bfloat16)
    for k in range(1, V):
        beta_copy(k).start()
    bbuf[me] = bsend[...]

    @pl.loop(0, etiles)
    def _(t):
        unit[pl.ds(pl.multiple_of(t * LANES, LANES), LANES), :] = (
            resid[t] * column(t)[:, :1]
        ).astype(jnp.bfloat16)

    home = me // group

    @pl.loop(0, groups)
    def _(q):
        slab = lax.rem(home + q, groups)
        for b in range(group):
            v = slab * group + b

            @pl.when(v != me)
            def _():
                remote(gt_ref, gbuf.at[v], gs.at[0], gr.at[v], "var", v).wait_recv()
                remote(bsend, bbuf.at[v], bs.at[0], br.at[v], "var", v).wait_recv()

            fit_in = bbuf[v]
            scale = fit_in[:, DESIGN:DESIGN + 1].astype(jnp.float32)
            scale = scale + fit_in[:, DESIGN + 1:DESIGN + 2].astype(jnp.float32)
            fitted = lax.dot_general(fit_in, d_ref[...], NN, preferred_element_type=jnp.float32)
            source[b * vb:(b + 1) * vb, :] = (
                (gbuf[v].astype(jnp.float32) - fitted) * scale
            ).astype(jnp.bfloat16)

        @pl.loop(0, S)
        def _(i):
            rows = pl.ds(pl.multiple_of(i * chunk, 16), chunk)
            term = lax.dot_general(unit[rows, :], source[...], NT, preferred_element_type=jnp.float32)
            terms[slab, rows, :] = term.astype(jnp.bfloat16)

        for k in range(1, S):
            p = samp_peer(k)
            part = terms.at[slab, pl.ds(pl.multiple_of(p * chunk, 16), chunk)]
            remote(part, terms_in.at[slab, mine], ts.at[slab, k], tr.at[slab, mine], "samp", p).start()

    width = group * vb
    own_rows = pl.ds(pl.multiple_of(mine * chunk, 16), chunk)

    @pl.loop(0, groups)
    def _(q):
        slab = lax.rem(home + q, groups)
        total = terms[slab, own_rows, :].astype(jnp.float32)
        for k in range(1, S):
            p = samp_peer(k)
            remote(terms.at[slab, own_rows], terms_in.at[slab, p], ts.at[slab, k], tr.at[slab, p],
                   "samp", p).wait_recv()
            total = total + terms_in[slab, p].astype(jnp.float32)
        out_ref[:, pl.ds(pl.multiple_of(slab * width, LANES), width)] = total

    for k in range(1, S):
        gram_copy(k).wait_send()
        cross_copy(k).wait_send()
        norm_copy(k).wait_send()
    for k in range(1, V):
        block_copy(k).wait_send()
        beta_copy(k).wait_send()

    @pl.loop(0, groups)
    def _(slab):
        for k in range(1, S):
            remote(terms.at[slab, own_rows], terms_in.at[slab, mine], ts.at[slab, k],
                   tr.at[slab, mine], "samp", samp_peer(k)).wait_send()


def correlate(expression, genotypes, covariates):
    S, V = lax.axis_size("samp"), lax.axis_size("var")
    samples, genes = expression.shape
    vb = genotypes.shape[1]
    gp = round_up(vb, LANES)
    group = math.lcm(vb, LANES) // vb
    groups = V // group
    tiles = (genes + gp) // LANES
    nrows = round_up(tiles, 8)
    design = jnp.concatenate(
        [jnp.ones((1, samples), jnp.bfloat16), covariates.T,
         jnp.zeros((LANES - DESIGN, samples), jnp.bfloat16)], axis=0)
    gt = genotypes.T
    xg = jnp.pad(gt, ((0, gp - vb), (0, 0)))
    chunk = genes // S
    bf, f32 = jnp.bfloat16, jnp.float32
    dma = pltpu.SemaphoreType.DMA
    return pl.pallas_call(
        functools.partial(kernel, S, V),
        out_shape=jax.ShapeDtypeStruct((chunk, V * vb), f32),
        in_specs=[pl.BlockSpec(memory_space=pltpu.VMEM)] * 4,
        out_specs=pl.BlockSpec(memory_space=pltpu.VMEM),
        scratch_shapes=[
            pltpu.VMEM((V, vb, samples), bf),
            pltpu.VMEM((V, vb, LANES), bf),
            pltpu.VMEM((gp // LANES, LANES, LANES), bf),
            pltpu.VMEM((vb, LANES), bf),
            pltpu.VMEM((DROWS, LANES), f32),
            pltpu.VMEM((S, DROWS, LANES), f32),
            pltpu.VMEM((tiles, DROWS, LANES), f32),
            pltpu.VMEM((S, tiles, DROWS, LANES), f32),
            pltpu.VMEM((tiles, LANES, samples), f32),
            pltpu.VMEM((nrows, LANES), f32),
            pltpu.VMEM((S, nrows, LANES), f32),
            pltpu.VMEM((nrows, LANES), f32),
            pltpu.VMEM((genes, samples), bf),
            pltpu.VMEM((group * vb, samples), bf),
            pltpu.VMEM((groups, genes, group * vb), bf),
            pltpu.VMEM((groups, S, chunk, group * vb), bf),
            dma((V,)), dma((V,)), dma((V,)), dma((V,)),
            dma((S,)), dma((S,)), dma((S,)), dma((S,)), dma((S,)), dma((S,)),
            dma((groups, S)), dma((groups, S)),
        ],
        compiler_params=pltpu.CompilerParams(
            collective_id=0, has_side_effects=True, vmem_limit_bytes=60 * 1024 * 1024),
    )(expression.T, xg, gt, design)


def shards(expression, genotypes, covariates, distance_bins, gene_folds, fold_weights):
    samples = expression.shape[0] * lax.axis_size("samp")
    corr = correlate(expression, genotypes, covariates)
    local_genes = corr.shape[0]
    fold_onehot = (gene_folds[:, None] == jnp.arange(FOLDS)[None, :]).astype(jnp.float32)
    row_weights = jnp.dot(fold_onehot, fold_weights, precision=lax.Precision.HIGHEST)
    bin_match = distance_bins.T[:, :, None] == jnp.arange(NBINS)[None, None, :]
    tile_weight = jnp.sum(jnp.where(bin_match, row_weights[:, None, :], 0.0), axis=2)
    dof = jnp.float32(samples - COVS - 2)
    stats = dof * corr * corr
    weighted = stats.reshape(local_genes, VTILES, VTILE) * tile_weight[:, :, None]
    return weighted.reshape(local_genes, VARS)


def solution(mesh):
    return jax.shard_map(
        shards,
        mesh=mesh,
        in_specs=(
            P(("groups", "samp"), "var"),
            P(("groups", "samp"), "var"),
            P(("groups", "samp"), None),
            P("groups", ("var", "samp")),
            P(("groups", "var", "samp")),
            P(),
        ),
        out_specs=P(("groups", "var", "samp"), None),
        check_vma=False,
    )
```

time: 192 us -> 116 us (0.60)
  waiting for transfers between devices: 109 us -> 0 us
  Pallas kernels: 0 us -> 104 us
  matrix products: 27.5 us -> 0.88 us
  blocking collectives: 20.9 us -> 0 us
  between operations: 13.2 us -> 0.03 us
  other arithmetic: 14.7 us -> 4.96 us
    pallas_call x0 -> x1, Pallas kernels: none -> 104 us  [correlate(): pl.pallas_call(functools.partial(kernel, S, V), out_shape=jax.ShapeDtypeS...]
    reduce_scatter x1 -> x0, waiting for transfers between devices: 42.2 us -> none  [shards(): corr = lax.psum_scatter(terms, 'samp', scatter_dimension=0, tiled=True)]
    all_gather x1 -> x0, waiting for transfers between devices: 40.7 us -> none  [shards(): source = lax.all_gather(genotypes, 'var', axis=1, tiled=True)]
    psum x1 -> x0, waiting for transfers between devices: 25.1 us -> none  [shards(): lax.psum((partial_sums[0], partial_sums[1], partial_sums[2]), 'samp')]
    dot_general x6 -> x0, matrix products: 23.5 us -> none  [the longest x2 8.07 us: solve_fit(): jnp.dot(design.astype(jnp.float32), beta, precision=lax.Precision.HIGHEST)]
    psum x2 -> x0, blocking collectives: 20.9 us -> none  [the longest x1 10.7 us: shards(): lax.psum((partial_sums[0], partial_sums[1], partial_sums[2]), 'samp')]
    another operation x5 -> x0, other arithmetic: 12.2 us -> none  [the longest x3 6.64 us: shards(): factor = jnp.linalg.cholesky(gram)]
    another operation x4 -> x0, matrix products: 3.86 us -> none  [solve_fit(): beta = jax.scipy.linalg.cho_solve((factor, True), cross)]
  transfers between devices with their start and end apart: 3 -> 0, of which waited for: 3 -> 0; matrix products, arithmetic and copies ran while one was open for 11% -> 0% of each run, Pallas kernels for 0% -> 0%
where the time goes in v1:
time: 116 us; the launch traced here: 115 us
  Pallas kernels  104 us (90%)
  local copies, waits for them, and re-layouts  5.21 us (4%)
  other arithmetic  4.96 us (4%)
    pallas_call x1, Pallas kernels, correlate(): pl.pallas_call(functools.partial(kernel, S, V), out_shape=jax.ShapeDtypeS...  104 us
    mul x1, other arithmetic, shards(): stats.reshape(local_genes, VTILES, VTILE) * tile_weight[:, :, None]  2.34 us

profile of v1, /device:TPU:13, one launch (start us, length us, event | category | flops | bytes accessed | tf_op | source)
XLA Modules:
  0.0 115.3 jit_solution(15662532726752639341)
XLA Ops:
  0.0 0.0 copy-start
  0.0 0.0 copy-start.1
  0.0 0.1 pad.7.clone
  0.1 0.6 copy-done
  0.7 0.9 fusion.1
  1.6 0.9 select_reduce_fusion
  2.5 0.1 copy.14
  2.6 1.7 %maximum_maximum_fusion.d_ref = bf16[128,1024]{1,0:T(8,128)(2,1)} fusion(bf16[64,1024]{1,0:T(8,128)(2,1)} %bitcast.9, bf16[128]{0:T(256)(128)(2,1)S(1)} %pad.7.clone, bf16[128]{0:T(256)(128)(2,1)S(1)} %pad.5.clone), kind=kLoop, calls=%fused_computation.4 | loop fusion | flops 786432 | bytes 393728 | tf_op jit(solution)/shard_map/concatenate | solution.py:267
  4.3 1.8 %pad.4.xg_ref = bf16[256,1024]{1,0:T(8,128)(2,1)} pad(bf16[192,1024]{1,0:T(8,128)(2,1)} %bitcast.7, bf16[]{:T(256)} %constant.4.clone.1), padding=0_64x0_0 | pad | bytes 917506 | tf_op jit(solution)/shard_map/jit(_pad)/pad | solution.py:271
  6.1 0.0 copy-done.1
  6.1 1.5 %copy.13 = bf16[1024,640]{0,1:T(8,128)(2,1)} copy(bf16[1024,640]{1,0:T(8,128)(2,1)S(1)} %copy-done.1) | data formatting | bytes 2621440 | tf_op args[0]
  7.7 104.2 %shard_map.64 = f32[160,1536]{1,0:T(8,128)} custom-call(bf16[640,1024]{1,0:T(8,128)(2,1)} %bitcast.6, bf16[256,1024]{1,0:T(8,128)(2,1)} %pad.4.xg_ref, bf16[192,1024]{1,0:T(8,128)(2,1)} %bitcast.8, bf16[128,1024]{1,0:T(8,128)(2,1)} %maximum_maximum_fusion.d_ref), custom_call_target="tpu_custom_call" | custom-call | tf_op jit(solution)/shard_map/pallas_call | solution.py:275
  111.9 0.6 mul.23
  112.5 0.5 mul.24
  112.9 2.3 %fusion = f32[160,1536]{1,0:T(8,128)} fusion(f32[160,1536]{1,0:T(8,128)S(1)} %mul.24, f32[160,1536]{1,0:T(8,128)} %shard_map.64), kind=kLoop, calls=%fused_computation.1 | loop fusion | flops 737280 | bytes 2949120 | tf_op jit(solution)/shard_map/mul | solution.py:316
  (2 shorter events, 0.0 us)
Async XLA Ops:
  0.0 0.7 copy-start
  0.0 6.1 %copy-start.1 = (bf16[1024,640]{1,0:T(8,128)(2,1)S(1)}, bf16[1024,640]{1,0:T(8,128)(2,1)}, u32[]{:S(2)}) copy-start(bf16[1024,640]{1,0:T(8,128)(2,1)} %param.6) | copy-start | bytes 3932164

commit v2 on v1

--- a/solution.py
+++ b/solution.py
@@ -40,16 +40,12 @@
     valid = (rows < DESIGN) & (cols < DESIGN)
     start = jnp.where(valid, gram, 0.0)
 
-    def sweep(k, a):
-        row = jnp.sum(jnp.where(rows == k, a, 0.0), axis=0, keepdims=True)
-        col = jnp.sum(jnp.where(cols == k, a, 0.0), axis=1, keepdims=True)
-        pivot = jnp.sum(jnp.where(cols[:1] == k, row, 0.0), axis=1, keepdims=True)
-        inv = 1.0 / pivot
-        scaled = row * inv
-        a = jnp.where(cols == k, 0.0, a) - col * jnp.where(cols[:1] == k, inv, scaled)
-        return jnp.where(rows == k, jnp.where(cols[:1] == k, inv, scaled), a)
-
-    swept = lax.fori_loop(0, DESIGN, sweep, start)
+    swept = start
+    for k in range(DESIGN):
+        inv = 1.0 / swept[k:k + 1, k:k + 1]
+        col = swept[:, k:k + 1]
+        scaled = jnp.where(cols[:1] == k, inv, swept[k:k + 1, :] * inv)
+        swept = jnp.where(rows == k, scaled, jnp.where(cols == k, 0.0, swept) - col * scaled)
     return jnp.where(valid, swept, 0.0)
 
 

time: 116 us -> 116 us (level)
  no operation moved by 1% of the time
where the time goes in v2:
time: 116 us; the launch traced here: 115 us
  Pallas kernels  104 us (90%)
  local copies, waits for them, and re-layouts  5.21 us (4%)
  other arithmetic  4.96 us (4%)
    pallas_call x1, Pallas kernels, correlate(): pl.pallas_call(functools.partial(kernel, S, V), out_shape=jax.ShapeDtypeS...  104 us
    mul x1, other arithmetic, shards(): stats.reshape(local_genes, VTILES, VTILE) * tile_weight[:, :, None]  2.34 us

profile of v2, /device:TPU:13, one launch (start us, length us, event | category | flops | bytes accessed | tf_op | source)
XLA Modules:
  0.0 115.3 jit_solution(1820725369810618320)
XLA Ops:
  0.0 0.0 copy-start
  0.0 0.0 copy-start.1
  0.0 0.1 pad.7.clone
  0.1 0.6 copy-done
  0.7 0.9 fusion.1
  1.6 0.9 select_reduce_fusion
  2.5 0.1 copy.14
  2.6 1.7 %maximum_maximum_fusion.d_ref = bf16[128,1024]{1,0:T(8,128)(2,1)} fusion(bf16[64,1024]{1,0:T(8,128)(2,1)} %bitcast.9, bf16[128]{0:T(256)(128)(2,1)S(1)} %pad.7.clone, bf16[128]{0:T(256)(128)(2,1)S(1)} %pad.5.clone), kind=kLoop, calls=%fused_computation.4 | loop fusion | flops 786432 | bytes 393728 | tf_op jit(solution)/shard_map/concatenate | solution.py:263
  4.3 1.8 %pad.4.xg_ref = bf16[256,1024]{1,0:T(8,128)(2,1)} pad(bf16[192,1024]{1,0:T(8,128)(2,1)} %bitcast.7, bf16[]{:T(256)} %constant.4.clone.1), padding=0_64x0_0 | pad | bytes 917506 | tf_op jit(solution)/shard_map/jit(_pad)/pad | solution.py:267
  6.1 0.0 copy-done.1
  6.1 1.5 %copy.13 = bf16[1024,640]{0,1:T(8,128)(2,1)} copy(bf16[1024,640]{1,0:T(8,128)(2,1)S(1)} %copy-done.1) | data formatting | bytes 2621440 | tf_op args[0]
  7.7 104.2 %shard_map.64 = f32[160,1536]{1,0:T(8,128)} custom-call(bf16[640,1024]{1,0:T(8,128)(2,1)} %bitcast.6, bf16[256,1024]{1,0:T(8,128)(2,1)} %pad.4.xg_ref, bf16[192,1024]{1,0:T(8,128)(2,1)} %bitcast.8, bf16[128,1024]{1,0:T(8,128)(2,1)} %maximum_maximum_fusion.d_ref), custom_call_target="tpu_custom_call" | custom-call | tf_op jit(solution)/shard_map/pallas_call | solution.py:271
  111.9 0.6 mul.23
  112.5 0.5 mul.24
  112.9 2.3 %fusion = f32[160,1536]{1,0:T(8,128)} fusion(f32[160,1536]{1,0:T(8,128)S(1)} %mul.24, f32[160,1536]{1,0:T(8,128)} %shard_map.64), kind=kLoop, calls=%fused_computation.1 | loop fusion | flops 737280 | bytes 2949120 | tf_op jit(solution)/shard_map/mul | solution.py:312
  (2 shorter events, 0.0 us)
Async XLA Ops:
  0.0 0.7 copy-start
  0.0 6.1 %copy-start.1 = (bf16[1024,640]{1,0:T(8,128)(2,1)S(1)}, bf16[1024,640]{1,0:T(8,128)(2,1)}, u32[]{:S(2)}) copy-start(bf16[1024,640]{1,0:T(8,128)(2,1)} %param.6) | copy-start | bytes 3932164
